TPU v7x, 32 devices: a whole 2x2x4 slice. The times are simulated.
32 devices in a mesh: row: 2 (over x), col: 16 (over z, y, core).
Axes of the slice: x: 2, y: 2, z: 4, core: 2. Of those that a mesh axis runs over, the one named last changes fastest.
Arguments:
- factors: bfloat16 [96, 256, 1024], P('col'), may hold values from -0.796875 to 0.796875
- metric_root: bfloat16 [1024, 1024], P('row'), may hold values from -1 to 2, as said below
- occ_energy: float32 [96], replicated, may hold values from -3 to -0.5
- vir_energy: float32 [256], replicated, may hold values from 0.2 to 4
- orbital_slot: int32 [96], replicated, may hold values from 0 to 95, each once
- source_plan: int32 [2, 2, 4], P('row'), may hold values from 0 to 95, as said below
- pair_list: int32 [2, 16, 2, 24], P('row', 'col'), may hold values from -1 to 23, as said below
Outputs:
- gamma_fit: float32 [2, 256, 8, 1024], P('row', 'col')
Inputs may be any that keep to these rules, and one draw needn't show every extreme that they name: `metric_root`: Symmetric. `source_plan`: all entries are distinct orbitals. `pair_list`: each list holds 2 to 24 distinct codes k * 6 + l first and -1 in the remaining entries; in every draw some list is full.
All inputs are finite; a program needn't handle non-finite values.
Results may differ from a plain program's by a relative error of at most 0.003.
Values may be sent and summed in bfloat16 or wider, within the bound.
A program may use at most 128 MiB of HBM per device.

v0:
```python
from functools import partial
import jax
import jax.numpy as jnp
from jax import lax
from jax.sharding import PartitionSpec as P


def from_root(shard, axis, root):
    mine = lax.axis_index(axis) == root
    return lax.psum(jnp.where(mine, shard, jnp.zeros_like(shard)), axis)


def fetch_factor(factors, slot_index, owned_slots):
    holder = slot_index // owned_slots
    position = slot_index % owned_slots
    portion = lax.dynamic_index_in_dim(factors, position, 0, keepdims=False)
    return from_root(portion, "col", holder)


def masked_weights(sources, factors, source_energy, local_energy, vir_energy, pair_mask):
    integrals = jnp.einsum("kaq,lbq->klab", sources, factors, preferred_element_type=jnp.float32)
    denominator = (
        source_energy[:, None, None, None]
        + local_energy[None, :, None, None]
        - vir_energy[None, None, :, None]
        - vir_energy[None, None, None, :]
    )
    amplitude = integrals / denominator
    return ((2.0 * amplitude - jnp.swapaxes(amplitude, 2, 3)) * pair_mask[:, :, None, None]).astype(
        jnp.bfloat16
    )


def contract_rows(weights, factors, offset, length):
    return jnp.einsum("klab,lbq->akq", weights, factors, preferred_element_type=jnp.float32)


def fold_metric(flat_gamma, portion):
    return jnp.dot(flat_gamma, portion, preferred_element_type=jnp.float32)


def on_device(factors, metric_root, occ_energy, vir_energy, orbital_slot, source_plan, pair_list):
    owned_slots = factors.shape[0]
    virtual = factors.shape[1]
    aux_count = factors.shape[2]
    columns = lax.axis_size("col")
    steps_count = source_plan.shape[1]
    sources_count = source_plan.shape[2]
    occupied = occ_energy.shape[0]
    column = lax.axis_index("col")
    local_slots = column * owned_slots + jnp.arange(owned_slots, dtype=jnp.int32)
    local_match = orbital_slot[None, :] == local_slots[:, None]
    local_energy = jnp.sum(jnp.where(local_match, occ_energy[None, :], 0.0), axis=1)
    source_match = (
        source_plan[0][:, :, None] == jnp.arange(occupied, dtype=jnp.int32)[None, None, :]
    )
    source_energy = jnp.sum(jnp.where(source_match, occ_energy[None, None, :], 0.0), axis=2)
    source_slot = jnp.sum(jnp.where(source_match, orbital_slot[None, None, :], 0), axis=2)
    code_range = jnp.arange(sources_count * owned_slots, dtype=jnp.int32)
    share_rows = virtual // columns
    makers = []
    for s in range(steps_count):
        sources = jnp.stack(
            [fetch_factor(factors, source_slot[s, k], owned_slots) for k in range(sources_count)]
        )
        code_list = pair_list[0, 0, s]
        pair_mask = (
            jnp.any(code_list[:, None] == code_range[None, :], axis=0)
            .reshape(sources_count, owned_slots)
            .astype(jnp.float32)
        )
        weights = masked_weights(
            sources, factors, source_energy[s], local_energy, vir_energy, pair_mask
        )
        term = partial(contract_rows, weights, factors)
        makers.append(term)
    offset = jnp.int32(0)
    gamma_rows = lax.psum_scatter(
        jnp.concatenate(
            [maker(offset, share_rows * lax.axis_size("col")) for maker in makers], axis=1
        ),
        "col",
        scatter_dimension=0,
        tiled=True,
    )
    flat_gamma = gamma_rows.astype(jnp.bfloat16).reshape(
        share_rows * steps_count * sources_count, aux_count
    )
    fitted = fold_metric(flat_gamma, lax.all_gather(metric_root, "row", axis=0, tiled=True))
    return fitted.reshape(1, share_rows, steps_count * sources_count, aux_count)


def solution(mesh):
    in_specs = (
        P("col", None, None),
        P("row", None),
        P(),
        P(),
        P(),
        P("row", None, None),
        P("row", "col", None, None),
    )
    out_specs = P("row", "col", None, None)
    return jax.shard_map(
        on_device, mesh=mesh, in_specs=in_specs, out_specs=out_specs, check_vma=False
    )
```

profile of v0, /device:TPU:0, one launch (start us, length us, event | category | flops | bytes accessed | tf_op | source)
XLA Modules:
  0.0 309.9 jit_solution(2107653622613330632)
XLA Ops:
  7.4 0.9 select_reduce_fusion.2
  8.3 0.7 fusion.42
  24.3 4.4 %dynamic-slice_select_fusion.7 = (bf16[1,256,1024]{2,1,0:T(8,128)(2,1)}, bf16[1,256,1024]{2,1,0:T(8,128)(2,1)}, bf16[1,256,1024]{2,1,0:T(8,128)(2,1)}, bf16[1,25...) fusion(bf16[6,256,1024]{2,1,0:T(8,128)(2,1)} %param.7, ...), kind=kLoop, calls=%fused_computation.47 | loop fusion | flops 2097152 | bytes 8388648 | tf_op jit(solution)/shard_map/jit(_where)/select_n | solution.py:10
  28.7 0.0 copy-start.3
  28.7 0.0 copy-start.6
  28.7 0.0 copy-start.5
  28.7 0.0 copy-start.1
  28.8 0.0 all-reduce.3.cloned.1.call-update
  28.8 0.0 all-gather.2.cloned.1.call-start
  28.8 0.5 all-gather.2.cloned.1.call-update
  29.4 0.0 reduce-scatter.2.cloned.1.call-start
  29.4 0.2 select_reduce_fusion.1
  29.6 0.2 select_reduce_fusion
  29.8 0.1 fusion.36
  29.9 0.1 reshape.200
  30.0 0.1 reshape.201
  30.1 0.1 broadcast_add_fusion.1
  30.2 0.1 broadcast_subtract_fusion.1
  30.2 113.7 %all-reduce.3.cloned.1.call-done = (bf16[1,256,1024]{2,1,0:T(8,128)(2,1)}, bf16[1,256,1024]{2,1,0:T(8,128)(2,1)}, bf16[1,256,1024]{2,1,0:T(8,128)(2,1)}, bf16[1,...) async-done(((bf16[1,256,1024]{2,1,0:T(8,128)(2,1)}, ...) | async-done | bytes 4194320 | tf_op jit(solution)/shard_map/psum | solution.py:10
  143.9 6.8 %fusion.14 = f32[4,256,6,256]{3,1,2,0:T(8,128)} fusion(bf16[6,256,1024]{2,1,0:T(8,128)(2,1)S(1)} %copy-done.1, bf16[1,256,1024]{2,1,0:T(8,128)(2,1)} %get-tuple-element.9, bf16[1,256,1024]{2,1,0:T(8,128)(2,1)} %get-tuple-element.10, bf16[1,256,1024]{2,1,0:T(8,128)(2,1)} %get-tuple-element.11, bf16[1,256,1024]{2,1,0:T(8,128)(2,1)} %get-tuple-element.12), kind=kOutput, calls=%fused_computation.21 | convolution fusion | flops 3229614080 | bytes 11534336 | tf_op jit(solution)/shard_map/kaq,lbq->klab/dot_general | solution.py:21
  150.8 6.5 %copy.10 = f32[4,256,6,256]{1,3,2,0:T(8,128)} copy(f32[4,256,6,256]{3,1,2,0:T(8,128)} %fusion.14) | data formatting | bytes 12582912 | tf_op jit(solution)/shard_map/kaq,lbq->klab/dot_general | solution.py:21
  157.3 7.2 %fusion.12 = f32[4,256,1024,1]{2,1,3,0:T(8,128)S(1)} fusion(bf16[6,256,1024]{2,1,0:T(8,128)(2,1)S(1)} %copy-done.1, f32[4,256,6,256]{3,1,2,0:T(8,128)} %fusion.14, f32[4,256,6,256]{1,3,2,0:T(8,128)} %copy.10, f32[4,6]{1,0:T(4,128)S(1)} %reshape.200, f32[256]{0:T(256)S(1)} %copy-done.5, f32[4,6,256]{2,1,0:T(8,128)S(1)} %get-tuple-element.21), kind=kOutput, calls=%fused_computation.19 | convolution fusion | flops 3233808384 | bytes 19948640 | tf_op jit(solution)/shard_map/klab,lbq->akq/dot_general | solution.py:35
  164.6 4.6 %copy.19 = f32[4,256,1024,1]{2,0,1,3:T(4,128)} copy(f32[4,256,1024,1]{2,1,3,0:T(8,128)S(1)} %fusion.12) | data formatting | bytes 8388608 | tf_op jit(solution)/shard_map/klab,lbq->akq/dot_general | solution.py:35
  169.2 5.3 %fusion.10 = f32[4,256,6,256]{3,1,2,0:T(8,128)} fusion(bf16[6,256,1024]{2,1,0:T(8,128)(2,1)S(1)} %copy-done.1, bf16[1,256,1024]{2,1,0:T(8,128)(2,1)S(1)} %copy-done.7, bf16[1,256,1024]{2,1,0:T(8,128)(2,1)S(1)} %copy-done.8, bf16[1,256,1024]{2,1,0:T(8,128)(2,1)S(1)} %copy-done.9, bf16[1,256,1024]{2,1,0:T(8,128)(2,1)S(1)} %copy-done.10), kind=kOutput, calls=%fused_computation.17 | convolution fusion | flops 3229614080 | bytes 11534336 | tf_op jit(solution)/shard_map/kaq,lbq->klab/dot_general | solution.py:21
  174.6 6.5 %copy.11 = f32[4,256,6,256]{1,3,2,0:T(8,128)} copy(f32[4,256,6,256]{3,1,2,0:T(8,128)} %fusion.10) | data formatting | bytes 12582912 | tf_op jit(solution)/shard_map/kaq,lbq->klab/dot_general | solution.py:21
  181.1 7.4 %fusion.8 = f32[4,256,1024,1]{2,1,3,0:T(8,128)S(1)} fusion(bf16[6,256,1024]{2,1,0:T(8,128)(2,1)S(1)} %copy-done.1, f32[4,256,6,256]{3,1,2,0:T(8,128)} %fusion.10, f32[4,256,6,256]{1,3,2,0:T(8,128)} %copy.11, f32[4,6]{1,0:T(4,128)S(1)} %reshape.201, f32[4,6,256]{2,1,0:T(8,128)S(1)} %get-tuple-element.22, f32[256]{0:T(256)S(1)} %copy-done.5), kind=kOutput, calls=%fused_computation.15 | convolution fusion | flops 3233808384 | bytes 19948640 | tf_op jit(solution)/shard_map/klab,lbq->akq/dot_general | solution.py:35
  188.5 2.7 copy.18
  191.2 5.4 %pad_maximum_fusion = f32[256,8,1024]{2,1,0:T(8,128)} fusion(f32[256,4,1024]{2,1,0:T(4,128)S(1)} %bitcast.102, f32[256,4,1024]{2,1,0:T(4,128)S(1)} %bitcast.101), kind=kLoop, calls=%fused_computation | loop fusion | flops 2097152 | bytes 16777216 | tf_op jit(solution)/shard_map/concatenate | solution.py:79
  196.6 0.0 reduce-scatter.2.cloned.1.call-update
  196.6 0.0 all-gather.2.cloned.1.call-done
  196.7 102.8 %reduce-scatter.2.cloned.1.call-done = f32[16,8,1024]{2,1,0:T(8,128)} async-done(((f32[256,8,1024]{2,1,0:T(8,128)}), f32[16,8,1024]{2,1,0:T(8,128)}) %reduce-scatter.2.cloned.1.call-update) | async-done | bytes 524304 | tf_op jit(solution)/shard_map/reduce_scatter | solution.py:78
  299.5 3.0 fusion.32
  (24 shorter events, 0.1 us)
Async XLA Ops:
  7.4 136.5 %all-reduce.3.cloned.1.call-start = ((), (), s32[]{:S(2)}) async-start(), calls=%async_computation.3 | async-start | bytes 8388608 | tf_op jit(solution)/shard_map/psum | solution.py:10
  28.7 0.7 copy-start.2
  28.7 0.7 copy-start.4
  28.7 0.9 copy-start.3
  28.7 1.1 copy-start.6
  28.7 1.4 copy-start.5
  28.7 115.2 %copy-start.1 = (bf16[6,256,1024]{2,1,0:T(8,128)(2,1)S(1)}, bf16[6,256,1024]{2,1,0:T(8,128)(2,1)}, u32[]{:S(2)}) copy-start(bf16[6,256,1024]{2,1,0:T(8,128)(2,1)} %param.7) | copy-start | bytes 9437188
  28.8 167.9 %all-gather.2.cloned.1.call-start = ((), (), s32[]{:S(2)}) async-start(), calls=%async_computation.2 | async-start | bytes 3145728 | tf_op jit(solution)/shard_map/all_gather | solution.py:89
  29.4 270.1 %reduce-scatter.2.cloned.1.call-start = ((), (), s32[]{:S(2)}) async-start(), calls=%async_computation.1 | async-start | bytes 8912896 | tf_op jit(solution)/shard_map/reduce_scatter | solution.py:78
  164.5 4.7 %copy-start.7 = (bf16[1,256,1024]{2,1,0:T(8,128)(2,1)S(1)}, bf16[1,256,1024]{2,1,0:T(8,128)(2,1)}, u32[]{:S(2)}) copy-start(bf16[1,256,1024]{2,1,0:T(8,128)(2,1)} %get-tuple-element.5) | copy-start | bytes 1572868
  164.5 4.7 %copy-start.8 = (bf16[1,256,1024]{2,1,0:T(8,128)(2,1)S(1)}, bf16[1,256,1024]{2,1,0:T(8,128)(2,1)}, u32[]{:S(2)}) copy-start(bf16[1,256,1024]{2,1,0:T(8,128)(2,1)} %get-tuple-element.6) | copy-start | bytes 1572868
  164.5 4.7 %copy-start.9 = (bf16[1,256,1024]{2,1,0:T(8,128)(2,1)S(1)}, bf16[1,256,1024]{2,1,0:T(8,128)(2,1)}, u32[]{:S(2)}) copy-start(bf16[1,256,1024]{2,1,0:T(8,128)(2,1)} %get-tuple-element.7) | copy-start | bytes 1572868
  164.6 4.7 %copy-start.10 = (bf16[1,256,1024]{2,1,0:T(8,128)(2,1)S(1)}, bf16[1,256,1024]{2,1,0:T(8,128)(2,1)}, u32[]{:S(2)}) copy-start(bf16[1,256,1024]{2,1,0:T(8,128)(2,1)} %get-tuple-element.8) | copy-start | bytes 1572868
  188.5 2.7 copy-start
Sparse Core Ops, SparseCore 0:
  28.9 114.9 all-reduce.2
  196.7 102.7 reduce-scatter.1
Sparse Core Ops, SparseCore 1:
  30.8 35.8 all-gather.1
where the time goes:
time: 310 us
  waiting for transfers between devices  217 us (70%)
  between operations  30.4 us (10%)
  matrix products  29.8 us (10%)
  local copies, waits for them, and re-layouts  21.3 us (7%)
  other arithmetic  11.2 us (4%)
    psum x1, waiting for transfers between devices, from_root(): return lax.psum(jnp.where(mine, shard, jnp.zeros_like(shard)), axis)  114 us
    reduce_scatter x1, waiting for transfers between devices, on_device(): lax.psum_scatter(jnp.concatenate([maker(offset, share_rows * lax.axis_siz...  103 us
    dot_general x2, matrix products, contract_rows(): jnp.einsum('klab,lbq->akq', weights, factors, preferred_element_type=jnp....  14.6 us
    dot_general x2, local copies, waits for them, and re-layouts, masked_weights(): jnp.einsum('kaq,lbq->klab', sources, factors, preferred_element_type=jnp....  13.1 us
    dot_general x2, matrix products, masked_weights(): jnp.einsum('kaq,lbq->klab', sources, factors, preferred_element_type=jnp....  12.2 us
    dot_general x2, local copies, waits for them, and re-layouts, contract_rows(): jnp.einsum('klab,lbq->akq', weights, factors, preferred_element_type=jnp....  7.33 us
  transfers between devices with their start and end apart: 3, of which 2 were waited for; matrix products, arithmetic and copies ran while one was open for 17% of the time, Pallas kernels for 0%

commit v1 on v0

--- a/solution.py
+++ b/solution.py
@@ -7,7 +7,7 @@
 
 def from_root(shard, axis, root):
     mine = lax.axis_index(axis) == root
-    return lax.psum(jnp.where(mine, shard, jnp.zeros_like(shard)), axis)
+    return jnp.sum(lax.all_gather(jnp.where(mine, shard, jnp.zeros_like(shard)), axis), axis=0)
 
 
 def fetch_factor(factors, slot_index, owned_slots):

time: 310 us -> 787 us (2.54)
  waiting for transfers between devices: 217 us -> 645 us
  other arithmetic: 11.2 us -> 64.4 us
    all_gather x0 -> x8, waiting for transfers between devices: none -> 539 us  [from_root(): lax.all_gather(jnp.where(mine, shard, jnp.zeros_like(shard)), axis)]
    psum x1 -> x0, waiting for transfers between devices: 114 us -> none  [from_root(): return lax.psum(jnp.where(mine, shard, jnp.zeros_like(shard)), axis)]
    reduce_sum x0 -> x8, other arithmetic: none -> 50.8 us  [from_root(): jnp.sum(lax.all_gather(jnp.where(mine, shard, jnp.zeros_like(shard)), axi...]
  transfers between devices with their start and end apart: 3 -> 10, of which waited for: 2 -> 9; matrix products, arithmetic and copies ran while one was open for 17% -> 8% of each run, Pallas kernels for 0% -> 0%
where the time goes in v1:
time: 787 us; the launch traced here: 786 us
  waiting for transfers between devices  645 us (82%)
  other arithmetic  64.4 us (8%)
  matrix products  30.9 us (4%)
  between operations  29.9 us (4%)
  local copies, waits for them, and re-layouts  15.4 us (2%)
    all_gather x8, waiting for transfers between devices, from_root(): lax.all_gather(jnp.where(mine, shard, jnp.zeros_like(shard)), axis)  539 us
    reduce_scatter x1, waiting for transfers between devices, on_device(): lax.psum_scatter(jnp.concatenate([maker(offset, share_rows * lax.axis_siz...  102 us
    reduce_sum x8, other arithmetic, from_root(): jnp.sum(lax.all_gather(jnp.where(mine, shard, jnp.zeros_like(shard)), axi...  50.8 us
  transfers between devices with their start and end apart: 10, of which 9 were waited for; matrix products, arithmetic and copies ran while one was open for 8% of the time, Pallas kernels for 0%

profile of v1, /device:TPU:0, one launch (start us, length us, event | category | flops | bytes accessed | tf_op | source)
XLA Modules:
  0.0 786.0 jit_solution(7976282774788656159)
XLA Ops:
  7.4 0.9 select_reduce_fusion.2
  24.1 4.3 dynamic-slice_select_fusion.7
  28.6 0.7 all-gather.16.cloned.1.call-update
  31.8 0.7 all-gather.22.cloned.1.call-update
  32.5 0.7 all-gather.24.cloned.1.call-update
  34.1 71.5 %all-gather.14.cloned.1.call-done = bf16[16,256,1024]{2,1,0:T(8,128)(2,1)} async-done(((bf16[1,256,1024]{2,1,0:T(8,128)(2,1)}), bf16[16,256,1024]{2,1,0:T(8,128)(2,1)}) %all-gather.14.cloned.1.call-update) | async-done | bytes 8388624 | tf_op jit(solution)/shard_map/all_gather | solution.py:10
  105.6 6.3 reduce_sum.126
  112.0 68.7 %all-gather.16.cloned.1.call-done = bf16[16,256,1024]{2,1,0:T(8,128)(2,1)} async-done(((bf16[1,256,1024]{2,1,0:T(8,128)(2,1)}), bf16[16,256,1024]{2,1,0:T(8,128)(2,1)}) %all-gather.16.cloned.1.call-update) | async-done | bytes 8388624 | tf_op jit(solution)/shard_map/all_gather | solution.py:10
  180.7 6.3 reduce_sum.127
  187.1 68.7 %all-gather.10.cloned.1.call-done = bf16[16,256,1024]{2,1,0:T(8,128)(2,1)} async-done(((bf16[1,256,1024]{2,1,0:T(8,128)(2,1)}), bf16[16,256,1024]{2,1,0:T(8,128)(2,1)}) %all-gather.10.cloned.1.call-update) | async-done | bytes 8388624 | tf_op jit(solution)/shard_map/all_gather | solution.py:10
  255.8 6.3 reduce_sum.124
  262.1 68.6 %all-gather.12.cloned.1.call-done = bf16[16,256,1024]{2,1,0:T(8,128)(2,1)} async-done(((bf16[1,256,1024]{2,1,0:T(8,128)(2,1)}), bf16[16,256,1024]{2,1,0:T(8,128)(2,1)}) %all-gather.12.cloned.1.call-update) | async-done | bytes 8388624 | tf_op jit(solution)/shard_map/all_gather | solution.py:10
  330.7 6.3 reduce_sum.125
  337.1 6.9 fusion.14
  344.0 6.6 copy.12
  350.6 55.1 %all-gather.18.cloned.1.call-done = bf16[16,256,1024]{2,1,0:T(8,128)(2,1)} async-done(((bf16[1,256,1024]{2,1,0:T(8,128)(2,1)}), bf16[16,256,1024]{2,1,0:T(8,128)(2,1)}) %all-gather.18.cloned.1.call-update) | async-done | bytes 8388624 | tf_op jit(solution)/shard_map/all_gather | solution.py:10
  405.6 6.3 reduce_sum.130
  412.0 68.6 %all-gather.20.cloned.1.call-done = bf16[16,256,1024]{2,1,0:T(8,128)(2,1)} async-done(((bf16[1,256,1024]{2,1,0:T(8,128)(2,1)}), bf16[16,256,1024]{2,1,0:T(8,128)(2,1)}) %all-gather.20.cloned.1.call-update) | async-done | bytes 8388624 | tf_op jit(solution)/shard_map/all_gather | solution.py:10
  480.6 6.4 reduce_sum.131
  487.0 68.7 %all-gather.22.cloned.1.call-done = bf16[16,256,1024]{2,1,0:T(8,128)(2,1)} async-done(((bf16[1,256,1024]{2,1,0:T(8,128)(2,1)}), bf16[16,256,1024]{2,1,0:T(8,128)(2,1)}) %all-gather.22.cloned.1.call-update) | async-done | bytes 8388624 | tf_op jit(solution)/shard_map/all_gather | solution.py:10
  555.6 6.4 reduce_sum.132
  562.0 68.7 %all-gather.24.cloned.1.call-done = bf16[16,256,1024]{2,1,0:T(8,128)(2,1)} async-done(((bf16[1,256,1024]{2,1,0:T(8,128)(2,1)}), bf16[16,256,1024]{2,1,0:T(8,128)(2,1)}) %all-gather.24.cloned.1.call-update) | async-done | bytes 8388624 | tf_op jit(solution)/shard_map/all_gather | solution.py:10
  630.7 6.3 reduce_sum.133
  637.1 6.8 fusion.10
  643.9 6.7 copy.14
  650.6 8.2 %fusion.18 = f32[256,4,1024]{2,0,1:T(8,128)S(1)} fusion(bf16[6,256,1024]{2,1,0:T(8,128)(2,1)} %param.7, f32[4,256,6,256]{3,1,2,0:T(8,128)} %fusion.14, f32[4,256,6,256]{1,3,2,0:T(8,128)} %copy.12, f32[4,6]{1,0:T(4,128)S(1)} %reshape.168, f32[256]{0:T(256)S(1)} %copy-done.6, f32[4,6,256]{2,1,0:T(8,128)S(1)} %get-tuple-element.13), kind=kOutput, calls=%fused_computation.21 | convolution fusion | flops 3233808384 | bytes 19948640 | tf_op jit(solution)/shard_map/klab,lbq->akq/dot_general | solution.py:35
  659.2 0.9 copy-done.2
  660.1 5.9 fusion.23
  666.0 6.7 pad_maximum_fusion
  673.3 101.5 %reduce-scatter.2.cloned.1.call-done = f32[16,8,1024]{2,0,1:T(8,128)} async-done(((f32[256,8,1024]{2,0,1:T(8,128)}), f32[16,8,1024]{2,0,1:T(8,128)}) %reduce-scatter.2.cloned.1.call-update) | async-done | bytes 524304 | tf_op jit(solution)/shard_map/reduce_scatter | solution.py:78
  774.8 1.1 convert_element_type.51
  776.0 2.9 fusion.42
  (51 shorter events, 5.0 us)
Async XLA Ops:
  7.4 98.3 %all-gather.14.cloned.1.call-start = ((), (), s32[]{:S(2)}) async-start(), calls=%async_computation.3 | async-start | bytes 8912896 | tf_op jit(solution)/shard_map/all_gather | solution.py:10
  28.5 4.8 copy-start.7
  28.5 5.1 copy-start.3
  28.5 5.1 copy-start.5
  28.5 5.3 copy-start.4
  28.5 5.5 copy-start.6
  28.5 152.2 %all-gather.16.cloned.1.call-start = ((), (), s32[]{:S(2)}) async-start(), calls=%async_computation.4 | async-start | bytes 8912896 | tf_op jit(solution)/shard_map/all_gather | solution.py:10
  29.3 226.5 %all-gather.10.cloned.1.call-start = ((), (), s32[]{:S(2)}) async-start(), calls=%async_computation.1 | async-start | bytes 8912896 | tf_op jit(solution)/shard_map/all_gather | solution.py:10
  30.0 300.7 %all-gather.12.cloned.1.call-start = ((), (), s32[]{:S(2)}) async-start(), calls=%async_computation.2 | async-start | bytes 8912896 | tf_op jit(solution)/shard_map/all_gather | solution.py:10
  30.6 375.1 %all-gather.18.cloned.1.call-start = ((), (), s32[]{:S(2)}) async-start(), calls=%async_computation.5 | async-start | bytes 8912896 | tf_op jit(solution)/shard_map/all_gather | solution.py:10
  31.2 449.4 %all-gather.20.cloned.1.call-start = ((), (), s32[]{:S(2)}) async-start(), calls=%async_computation.6 | async-start | bytes 8912896 | tf_op jit(solution)/shard_map/all_gather | solution.py:10
  31.7 523.9 %all-gather.22.cloned.1.call-start = ((), (), s32[]{:S(2)}) async-start(), calls=%async_computation.7 | async-start | bytes 8912896 | tf_op jit(solution)/shard_map/all_gather | solution.py:10
  32.5 598.2 %all-gather.24.cloned.1.call-start = ((), (), s32[]{:S(2)}) async-start(), calls=%async_computation.8 | async-start | bytes 8912896 | tf_op jit(solution)/shard_map/all_gather | solution.py:10
  33.2 741.6 %reduce-scatter.2.cloned.1.call-start = ((), (), s32[]{:S(2)}) async-start(), calls=%async_computation.9 | async-start | bytes 8912896 | tf_op jit(solution)/shard_map/reduce_scatter | solution.py:78
  262.1 74.9 %copy-start.1 = (bf16[6,256,1024]{2,1,0:T(8,128)(2,1)S(1)}, bf16[6,256,1024]{2,1,0:T(8,128)(2,1)}, u32[]{:S(2)}) copy-start(bf16[6,256,1024]{2,1,0:T(8,128)(2,1)} %param.7) | copy-start | bytes 9437188
  643.9 15.0 %slice-start = ((s8[6291456]{0:T(1024)(128)(4,1)}), s8[2097152]{0:T(1024)(128)(4,1)S(1)}, s32[]{:S(2)}) async-start(s8[6291456]{0:T(1024)(128)(4,1)} %bitcast.121), calls=%async_computation.11 | async-start | bytes 4194304
  650.6 8.3 %slice-start.1 = ((s8[6291456]{0:T(1024)(128)(4,1)}), s8[4194304]{0:T(1024)(128)(4,1)S(1)}, s32[]{:S(2)}) async-start(s8[6291456]{0:T(1024)(128)(4,1)} %bitcast.121), calls=%async_computation.12 | async-start | bytes 8388608
  650.6 8.6 %copy-start = (f32[4,256,6,256]{1,3,2,0:T(8,128)S(1)}, f32[4,256,6,256]{1,3,2,0:T(8,128)}, u32[]{:S(2)}) copy-start(f32[4,256,6,256]{1,3,2,0:T(8,128)} %copy.14) | copy-start | bytes 18874372
  650.6 9.5 %copy-start.2 = (bf16[6,256,1024]{2,1,0:T(8,128)(2,1)S(1)}, bf16[6,256,1024]{2,1,0:T(8,128)(2,1)}, u32[]{:S(2)}) copy-start(bf16[6,256,1024]{2,1,0:T(8,128)(2,1)} %param.7) | copy-start | bytes 9437188
  672.7 103.2 %all-gather.26.cloned.1.call-start = ((), (), s32[]{:S(2)}) async-start(), calls=%async_computation.10 | async-start | bytes 3145728 | tf_op jit(solution)/shard_map/all_gather | solution.py:89
Sparse Core Ops, SparseCore 0:
  28.6 76.9 all-gather.13
  107.8 72.8 all-gather.15
  182.9 72.8 all-gather.9
  257.8 72.8 all-gather.11
  332.7 72.8 all-gather.17
  407.7 72.8 all-gather.19
  482.7 72.8 all-gather.21
  557.8 72.8 all-gather.23
  672.8 101.9 reduce-scatter.1
Sparse Core Ops, SparseCore 1:
  674.7 31.5 all-gather.25
